TPU v7x, 512 devices: a whole 4x8x8 slice. The times are simulated.
512 devices in a mesh: dp: 4 (over x), seq: 16 (over z, core), tensor: 8 (over y).
Axes of the slice: x: 4, y: 8, z: 8, core: 2. Of those that a mesh axis runs over, the one named last changes fastest.
Arguments:
- hidden: bfloat16 [8192, 8192], P(('dp', 'seq'), 'tensor'), may hold values from -6 to 6
- queries: bfloat16 [8192, 8192], P(('dp', 'seq'), 'tensor'), may hold values from -14 to 14
- kv_weight: bfloat16 [8192, 2048], P('seq', 'tensor'), may hold values from -0.0625 to 0.0625
- parents: int32 [4, 16], P('dp'), may hold values from -1 to 14, as said below
- out_grad: bfloat16 [8192, 8192], P(('dp', 'seq'), 'tensor'), may hold values from -6 to 6
Outputs:
- attended: bfloat16 [8192, 8192], P(('dp', 'seq'), 'tensor')
- query_grad: float32 [8192, 8192], P(('dp', 'seq'), 'tensor')
- weight_grad: float32 [8192, 2048], P('seq', 'tensor')
Inputs may be any that keep to these rules, and one draw needn't show every extreme that they name: parents[g, n] is -1 where node block n begins a new tree of group g (always for n = 0), else an earlier node block of the same group; the last node block of every group has parent 16 - 2.
All inputs are finite; a program needn't handle non-finite values.
Results may differ from a plain program's by a relative error of at most 0.012.
The roundings to bfloat16 on the way count: a program that leaves them out, or rounds other values in their place, can miss the bound.
Values may be sent and summed in bfloat16 or wider, within the bound.
No kernel may reach another device: no remote copies, remote signals or barrier semaphores. Data moves between devices by JAX's collectives and lax.ppermute only.
A program may use at most 64 MiB of HBM per device.

v0:
```python
import math
import jax
import jax.numpy as jnp
from jax import lax
from jax.sharding import PartitionSpec as P

HD = 128


def attend_block(query_blk, grad_blk, keys_head, values_head, visible):
    inv_root = 1.0 / math.sqrt(query_blk.shape[-1])
    scores = (
        jnp.einsum("thd,jd->htj", query_blk, keys_head, preferred_element_type=jnp.float32)
        * inv_root
    )
    scores = jnp.where(visible[None], scores, -jnp.inf)
    row_top = jnp.max(scores, axis=-1, keepdims=True)
    expons = jnp.exp(scores - row_top)
    probs_f = expons / jnp.sum(expons, axis=-1, keepdims=True)
    weights = probs_f.astype(jnp.bfloat16)
    mixed_f = jnp.einsum("htj,jd->thd", weights, values_head, preferred_element_type=jnp.float32)
    prob_grad = jnp.einsum("thd,jd->htj", grad_blk, values_head, preferred_element_type=jnp.float32)
    inner_sum = jnp.transpose(jnp.sum(grad_blk.astype(jnp.float32) * mixed_f, axis=-1), (1, 0))
    score_grad = (probs_f * (prob_grad - inner_sum[:, :, None]) * inv_root).astype(jnp.bfloat16)
    query_grad = jnp.einsum(
        "htj,jd->thd", score_grad, keys_head, preferred_element_type=jnp.float32
    )
    key_grad = jnp.einsum("htj,thd->jd", score_grad, query_blk, preferred_element_type=jnp.float32)
    value_grad = jnp.einsum("htj,thd->jd", weights, grad_blk, preferred_element_type=jnp.float32)
    return (mixed_f.astype(jnp.bfloat16), query_grad, key_grad, value_grad)


def per_device(hidden, queries, kv_weight, parents, out_grad):
    tok_rows = queries.shape[0]
    head_size = HD
    kv_local = kv_weight.shape[1] // (2 * head_size)
    heads_local = queries.shape[1] // head_size
    heads_per = heads_local // kv_local
    block_heads = max(1, min(heads_per, 512 // tok_rows))
    block_count = heads_per // block_heads
    node_count = lax.axis_size("seq")
    my_node = lax.axis_index("seq")
    group_rows = tok_rows * node_count
    whole_rows = lax.all_gather(hidden, "tensor", axis=1, tiled=True)
    traded = lax.all_to_all(whole_rows, "seq", split_axis=1, concat_axis=0, tiled=True)
    partial_kv = jnp.dot(traded, kv_weight, preferred_element_type=jnp.float32)
    kv_all = lax.psum(partial_kv, "seq").astype(jnp.bfloat16)
    parent_list = parents[0]
    node_ids = jnp.arange(node_count, dtype=jnp.int32)

    def follow(step_index, state_pair):
        current, marked = state_pair
        marked = jnp.maximum(marked, (node_ids == current).astype(jnp.int32))
        current = jnp.where(current >= 0, parent_list[jnp.maximum(current, 0)], -1)
        return (current, marked)

    start_pair = (parent_list[my_node], jnp.zeros((node_count,), jnp.int32))
    final_pair = lax.fori_loop(0, node_count, follow, start_pair)
    key_above = jnp.broadcast_to(final_pair[1][:, None] > 0, (node_count, tok_rows)).reshape(
        group_rows
    )
    key_node = jnp.arange(group_rows, dtype=jnp.int32) // tok_rows
    key_pos = jnp.arange(group_rows, dtype=jnp.int32) % tok_rows
    query_pos = jnp.arange(tok_rows, dtype=jnp.int32)
    visible = key_above[None, :] | (key_node == my_node)[None, :] & (
        key_pos[None, :] <= query_pos[:, None]
    )
    kv_heads = kv_all.reshape(group_rows, kv_local, 2, head_size).transpose(1, 0, 2, 3)
    query_split = queries.reshape(
        tok_rows, kv_local, block_count, block_heads, head_size
    ).transpose(1, 2, 0, 3, 4)
    grad_split = out_grad.reshape(
        tok_rows, kv_local, block_count, block_heads, head_size
    ).transpose(1, 2, 0, 3, 4)

    def per_head(packed):
        query_head, grad_head, head_kv = packed
        keys_head = head_kv[:, 0, :]
        values_head = head_kv[:, 1, :]

        def per_part(running, block_pair):
            mixed_blk, qgrad_blk, key_grad, value_grad = attend_block(
                block_pair[0], block_pair[1], keys_head, values_head, visible
            )
            return ((running[0] + key_grad, running[1] + value_grad), (mixed_blk, qgrad_blk))

        zero_grad = jnp.zeros((group_rows, head_size), jnp.float32)
        sums_pair, outputs = lax.scan(per_part, (zero_grad, zero_grad), (query_head, grad_head))
        return (outputs[0], outputs[1], jnp.stack([sums_pair[0], sums_pair[1]], axis=1))

    mixed_all, qgrad_all, kv_terms = lax.map(per_head, (query_split, grad_split, kv_heads))
    attended = mixed_all.transpose(2, 0, 1, 3, 4).reshape(tok_rows, heads_local * head_size)
    query_grad = qgrad_all.transpose(2, 0, 1, 3, 4).reshape(tok_rows, heads_local * head_size)
    kv_terms = kv_terms.transpose(1, 0, 2, 3).reshape(group_rows, kv_local * 2 * head_size)
    kv_grads = lax.psum(kv_terms.astype(jnp.bfloat16), "seq")
    local_weight = lax.dot_general(
        traded, kv_grads, (((0,), (0,)), ((), ())), preferred_element_type=jnp.float32
    )
    weight_grad = lax.psum(local_weight * (1.0 / (lax.axis_size("dp") * node_count)), "dp")
    return (attended, query_grad, weight_grad)


def solution(mesh):
    placed = (
        P(("dp", "seq"), "tensor"),
        P(("dp", "seq"), "tensor"),
        P("seq", "tensor"),
        P("dp", None),
        P(("dp", "seq"), "tensor"),
    )
    return jax.shard_map(
        per_device,
        mesh=mesh,
        in_specs=placed,
        out_specs=(P(("dp", "seq"), "tensor"), P(("dp", "seq"), "tensor"), P("seq", "tensor")),
        check_vma=False,
    )
```

profile of v0, /device:TPU:8, one launch (start us, length us, event | category | flops | bytes accessed | tf_op | source)
XLA Modules:
  0.0 414.3 jit_solution(17990220807136559389)
XLA Ops:
  7.2 1.8 copy.37
  10.3 1.8 copy.40
  12.1 1.3 constant_dynamic-slice_fusion.1
  13.4 45.1 %all-gather.2.cloned.1.call-done = bf16[128,8192]{0,1:T(8,128)(2,1)} async-done(((bf16[128,1024]{0,1:T(8,128)(2,1)}), bf16[128,8192]{0,1:T(8,128)(2,1)}) %all-gather.2.cloned.1.call-update) | async-done | bytes 2097168 | tf_op jit(solution)/shard_map/all_gather | solution.py:44
  58.4 7.5 %all-to-all-start = ((bf16[128,16,512]{0,2,1:T(8,128)(2,1)}), bf16[128,16,512]{0,2,1:T(8,128)(2,1)S(1)}, u32[]{:S(2)}, u32[]{:S(2)}) async-start(bf16[128,16,512]{0,2,1:T(8,128)(2,1)} %bitcast.163), calls=%async_computation | async-start | bytes 4194304 | tf_op jit(solution)/shard_map/all_to_all | solution.py:45
  66.0 40.3 %while.42 = (s32[]{:T(128)}, s32[]{:T(128)}, s32[16]{0:T(128)S(1)}, s32[16]{0:T(128)S(1)}, s32[]{:T(128)}, /*index=5*/s32[]{:T(128)}, s32[]{:T(128)}) while((s32[]{:T(128)}, s32[]{:T(128)}, s32[16]{0:T(128)S(1)}, s32[16]{0:T(128)S(1)}, s32[]{:T(128)}, /*index=5*/s32[]{:T(128)}, s32[]{:T(128)}) %tuple.73), condition=%wide.region_2.3_spmd.clone, body=%wide.region_1.2_spmd.clone.sunk | while | flops 70 | bytes 273 | solution.py:58
  106.4 8.8 %all-to-all-done = bf16[128,16,512]{0,2,1:T(8,128)(2,1)S(1)} async-done(((bf16[128,16,512]{0,2,1:T(8,128)(2,1)}), bf16[128,16,512]{0,2,1:T(8,128)(2,1)S(1)}, u32[]{:S(2)}, u32[]{:S(2)}) %all-to-all-start) | async-done | bytes 2097184 | tf_op jit(solution)/shard_map/all_to_all | solution.py:45
  115.2 1.3 copy-done.7
  116.5 2.9 copy.38
  119.4 2.0 fusion.48
  121.4 60.2 %all-reduce.7 = bf16[2048,256]{1,0:T(8,128)(2,1)} all-reduce(f32[2048,256]{1,0:T(8,128)} %fusion.48), channel_id=1, replica_groups=mesh['dp'=4,'seq'=16,'tensor'=8] {'seq'}, use_global_device_ids=true, to_apply=%region_0.0 | all-reduce | flops 524288 | bytes 3145728 | tf_op jit(solution)/shard_map/psum | solution.py:47
  181.6 2.2 squeeze.41
  183.8 3.2 fusion.47
  187.0 1.8 copy.57
  188.9 39.9 %while.43 = (s32[]{:T(128)}, f32[2048,128]{1,0:T(8,128)}, f32[2048,128]{1,0:T(8,128)}, bf16[2,128,4,128]{3,1,2,0:T(8,128)(2,1)}, f32[2,128,4,128]{3,1,2,0:T(8,12...) while((s32[]{:T(128)}, f32[2048,128]{1,0:T(8,128)}, ...), condition=%wide.region_7.8_spmd.clone, body=%wide.region_3.7_spmd.clone.sunk | while | flops 1626342912 | bytes 79985504 | solution.py:88
  189.8 1.9 fusion.91
  191.7 1.9 copy-done.2
  195.4 1.8 multiply_reduce_fusion.2
  197.2 4.5 %fusion.93 = bf16[4,128,2048]{2,1,0:T(8,128)(2,1)} fusion(f32[4,128]{1,0:T(4,128)S(1)} %bitcast.169, f32[4,128,2048]{2,1,0:T(8,128)} %copy-done.2, f32[4,128]{1,0:T(4,128)} %copy-done.11, bf16[2048,128]{0,1:T(8,128)(2,1)} %get-tuple-element.411, bf16[1,128,4,128]{1,3,2,0:T(8,128)(2,1)S(1)} %constant_dynamic-slice_fusion.3), kind=kOutput, calls=%fused_computation.9.clone.1 | convolution fusion | flops 273678336 | bytes 6950912 | tf_op jit(solution)/shard_map/while/body/eval_jaxpr/while/body/eval_jaxpr/thd,jd->htj/dot_general | solution.py:22
  201.8 3.5 fusion.94
  209.7 1.9 fusion.91
  211.6 1.9 copy-done.2
  215.2 1.8 multiply_reduce_fusion.2
  217.1 4.5 %fusion.93 = bf16[4,128,2048]{2,1,0:T(8,128)(2,1)} fusion(f32[4,128]{1,0:T(4,128)S(1)} %bitcast.169, f32[4,128,2048]{2,1,0:T(8,128)} %copy-done.2, f32[4,128]{1,0:T(4,128)} %copy-done.11, bf16[2048,128]{0,1:T(8,128)(2,1)} %get-tuple-element.411, bf16[1,128,4,128]{1,3,2,0:T(8,128)(2,1)S(1)} %constant_dynamic-slice_fusion.3), kind=kOutput, calls=%fused_computation.9.clone.1 | convolution fusion | flops 273678336 | bytes 6950912 | tf_op jit(solution)/shard_map/while/body/eval_jaxpr/while/body/eval_jaxpr/thd,jd->htj/dot_general | solution.py:22
  221.6 3.8 fusion.94
  228.8 1.6 copy.47
  230.4 1.4 copy.46
  233.0 116.3 %all-reduce.4.cloned.1.call-done = bf16[2048,256]{0,1:T(8,128)(2,1)} async-done(((bf16[2048,256]{0,1:T(8,128)(2,1)}), bf16[2048,256]{0,1:T(8,128)(2,1)}) %all-reduce.4.cloned.1.call-update) | async-done | bytes 1048592 | tf_op jit(solution)/shard_map/psum | solution.py:95
  349.3 2.7 fusion.37
  353.5 1.2 copy.44
  355.5 50.2 %all-reduce.6.cloned.1.call-done = f32[512,256]{0,1:T(8,128)} async-done(((f32[512,256]{0,1:T(8,128)}), f32[512,256]{0,1:T(8,128)}) %all-reduce.6.cloned.1.call-update) | async-done | bytes 524304 | tf_op jit(solution)/shard_map/psum | solution.py:99
  405.7 2.0 copy.48
  (106 shorter events, 26.4 us)
Async XLA Ops:
  7.2 112.2 %copy-start = (bf16[512,256]{1,0:T(8,128)(2,1)S(1)}, bf16[512,256]{1,0:T(8,128)(2,1)}, u32[]{:S(2)}) copy-start(bf16[512,256]{1,0:T(8,128)(2,1)} %param.11) | copy-start | bytes 786436
  7.2 58.8 %copy-start.12 = (s32[1,16]{1,0:T(1,128)S(1)}, s32[1,16]{1,0:T(1,128)}, u32[]{:S(2)}) copy-start(s32[1,16]{1,0:T(1,128)} %param.12) | copy-start | bytes 196
  7.2 51.3 %all-gather.2.cloned.1.call-start = ((), (), s32[]{:S(2)}) async-start(), calls=%async_computation.1 | async-start | bytes 2359296 | tf_op jit(solution)/shard_map/all_gather | solution.py:44
  58.4 56.7 %all-to-all-start = ((bf16[128,16,512]{0,2,1:T(8,128)(2,1)}), bf16[128,16,512]{0,2,1:T(8,128)(2,1)S(1)}, u32[]{:S(2)}, u32[]{:S(2)}) async-start(bf16[128,16,512]{0,2,1:T(8,128)(2,1)} %bitcast.163), calls=%async_computation | async-start | bytes 4194304 | tf_op jit(solution)/shard_map/all_to_all | solution.py:45
  65.9 283.4 %all-reduce.4.cloned.1.call-start = ((), (), s32[]{:S(2)}) async-start(), calls=%async_computation.2 | async-start | bytes 2097152 | tf_op jit(solution)/shard_map/psum | solution.py:95
  115.2 1.3 copy-start.7
  119.4 62.2 %copy-start.5 = (bf16[16,128,512]{2,1,0:T(8,128)(2,1)}, bf16[16,128,512]{2,1,0:T(8,128)(2,1)S(1)}, u32[]{:S(2)}) copy-start(bf16[16,128,512]{2,1,0:T(8,128)(2,1)S(1)} %copy.38) | copy-start | bytes 6291460
  191.7 2.0 copy-start.2
  191.7 2.6 copy-start.11
  201.8 3.6 copy-start.1
  201.8 3.6 copy-start.8
  201.8 4.3 %copy-start.3 = (f32[2048,128]{1,0:T(8,128)S(1)}, f32[2048,128]{1,0:T(8,128)}, u32[]{:S(2)}) copy-start(f32[2048,128]{1,0:T(8,128)} %get-tuple-element.391) | copy-start | bytes 3145732 | tf_op jit(solution)/shard_map/while/body/eval_jaxpr/while
  206.0 2.0 copy-start.9
  207.1 1.0 copy-start.4
  211.5 2.0 copy-start.2
  211.5 2.6 copy-start.11
  221.6 3.8 copy-start.1
  221.6 3.8 copy-start.8
  221.6 4.5 %copy-start.3 = (f32[2048,128]{1,0:T(8,128)S(1)}, f32[2048,128]{1,0:T(8,128)}, u32[]{:S(2)}) copy-start(f32[2048,128]{1,0:T(8,128)} %get-tuple-element.391) | copy-start | bytes 3145732 | tf_op jit(solution)/shard_map/while/body/eval_jaxpr/while
  226.1 2.0 copy-start.9
  227.2 1.0 copy-start.4
  228.8 120.5 %copy-start.6 = (bf16[16,128,512]{2,1,0:T(8,128)(2,1)S(1)}, bf16[16,128,512]{2,1,0:T(8,128)(2,1)}, u32[]{:S(2)}) copy-start(bf16[16,128,512]{2,1,0:T(8,128)(2,1)} %copy-done.5) | copy-start | bytes 6291460
  232.9 119.2 %copy-start.10 = (f32[2,128,4,128]{3,1,2,0:T(8,128)S(1)}, f32[2,128,4,128]{3,1,2,0:T(8,128)}, u32[]{:S(2)}) copy-start(f32[2,128,4,128]{3,1,2,0:T(8,128)} %get-tuple-element.111) | copy-start | bytes 1572868
  232.9 172.8 %all-reduce.6.cloned.1.call-start = ((), (), s32[]{:S(2)}) async-start(), calls=%async_computation.3 | async-start | bytes 1048576 | tf_op jit(solution)/shard_map/psum | solution.py:99
Sparse Core Ops, SparseCore 0:
  10.7 47.7 all-gather.1
  233.1 116.2 all-reduce.3
  352.2 53.4 all-reduce.5
where the time goes:
time: 415 us; the launch traced here: 414 us
  waiting for transfers between devices  220 us (53%)
  blocking collectives  60.2 us (15%)
  local copies, waits for them, and re-layouts  44.7 us (11%)
  loops' own time  30.9 us (7%)
  matrix products  29.8 us (7%)
  between operations  13.9 us (3%)
  starting transfers between devices  7.6 us (2%)
  other arithmetic  6.75 us (2%)
    psum x1, waiting for transfers between devices, per_device(): kv_grads = lax.psum(kv_terms.astype(jnp.bfloat16), 'seq')  116 us
    psum x1, blocking collectives, per_device(): kv_all = lax.psum(partial_kv, 'seq').astype(jnp.bfloat16)  60.2 us
    psum x1, waiting for transfers between devices, per_device(): lax.psum(local_weight * (1.0 / (lax.axis_size('dp') * node_count)), 'dp')  50.2 us
    all_gather x1, waiting for transfers between devices, per_device(): whole_rows = lax.all_gather(hidden, 'tensor', axis=1, tiled=True)  45.1 us
    another operation x1, loops' own time, per_device(): final_pair = lax.fori_loop(0, node_count, follow, start_pair)  30.7 us
    unnamed x18, local copies, waits for them, and re-layouts  10 us
    dynamic_slice x16, local copies, waits for them, and re-layouts, follow(): current = jnp.where(current >= 0, parent_list[jnp.maximum(current, 0)], -1)  9.39 us
    dot_general x2, matrix products, attend_block(): jnp.einsum('thd,jd->htj', grad_blk, values_head, preferred_element_type=j...  9.07 us
  transfers between devices with their start and end apart: 4, of which 4 were waited for; matrix products, arithmetic and copies ran while one was open for 4% of the time, Pallas kernels for 0%

commit v1 on v0

--- a/solution.py
+++ b/solution.py
@@ -41,7 +41,9 @@
     node_count = lax.axis_size("seq")
     my_node = lax.axis_index("seq")
     group_rows = tok_rows * node_count
-    whole_rows = lax.all_gather(hidden, "tensor", axis=1, tiled=True)
+    whole_rows = jnp.concatenate(
+        lax.all_to_all(jnp.stack([hidden] * lax.axis_size("tensor")), "tensor", 0, 0), axis=1
+    )
     traded = lax.all_to_all(whole_rows, "seq", split_axis=1, concat_axis=0, tiled=True)
     partial_kv = jnp.dot(traded, kv_weight, preferred_element_type=jnp.float32)
     kv_all = lax.psum(partial_kv, "seq").astype(jnp.bfloat16)

time: 415 us -> 426 us (1.027)
  starting transfers between devices: 7.6 us -> 20.5 us
    all_to_all x0 -> x1, waiting for transfers between devices: none -> 45.6 us  [per_device(): lax.all_to_all(jnp.stack([hidden] * lax.axis_size('tensor')), 'tensor', 0...]
    all_gather x1 -> x0, waiting for transfers between devices: 45.1 us -> none  [per_device(): whole_rows = lax.all_gather(hidden, 'tensor', axis=1, tiled=True)]
    all_to_all x0 -> x1, starting transfers between devices: none -> 10 us  [per_device(): lax.all_to_all(jnp.stack([hidden] * lax.axis_size('tensor')), 'tensor', 0...]
    unnamed x18 -> x22, local copies, waits for them, and re-layouts: 10 us -> 7.48 us
  transfers between devices with their start and end apart: 4 -> 4, of which waited for: 4 -> 4; matrix products, arithmetic and copies ran while one was open for 4% -> 3% of each run, Pallas kernels for 0% -> 0%
where the time goes in v1:
time: 426 us; the launch traced here: 425 us
  waiting for transfers between devices  221 us (52%)
  blocking collectives  60.2 us (14%)
  local copies, waits for them, and re-layouts  42.5 us (10%)
  loops' own time  29.8 us (7%)
  matrix products  29.8 us (7%)
  starting transfers between devices  20.5 us (5%)
  between operations  14.2 us (3%)
  other arithmetic  6.75 us (2%)
    psum x1, waiting for transfers between devices, per_device(): kv_grads = lax.psum(kv_terms.astype(jnp.bfloat16), 'seq')  115 us
    psum x1, blocking collectives, per_device(): kv_all = lax.psum(partial_kv, 'seq').astype(jnp.bfloat16)  60.2 us
    psum x1, waiting for transfers between devices, per_device(): lax.psum(local_weight * (1.0 / (lax.axis_size('dp') * node_count)), 'dp')  50.2 us
    all_to_all x1, waiting for transfers between devices, per_device(): lax.all_to_all(jnp.stack([hidden] * lax.axis_size('tensor')), 'tensor', 0...  45.6 us
    another operation x1, loops' own time, per_device(): final_pair = lax.fori_loop(0, node_count, follow, start_pair)  29.6 us
    all_to_all x1, starting transfers between devices, per_device(): lax.all_to_all(whole_rows, 'seq', split_axis=1, concat_axis=0, tiled=True)  10.4 us
    all_to_all x1, waiting for transfers between devices, per_device(): lax.all_to_all(whole_rows, 'seq', split_axis=1, concat_axis=0, tiled=True)  10.4 us
    all_to_all x1, starting transfers between devices, per_device(): lax.all_to_all(jnp.stack([hidden] * lax.axis_size('tensor')), 'tensor', 0...  10 us
  transfers between devices with their start and end apart: 4, of which 4 were waited for; matrix products, arithmetic and copies ran while one was open for 3% of the time, Pallas kernels for 0%

profile of v1, /device:TPU:8, one launch (start us, length us, event | category | flops | bytes accessed | tf_op | source)
XLA Modules:
  0.0 425.0 jit_solution(10208193679815595699)
XLA Ops:
  7.2 1.2 copy.22
  8.4 1.6 stack.26
  10.0 10.0 %all-to-all-start = ((bf16[8,128,1024]{1,2,0:T(8,128)(2,1)}), bf16[8,128,1024]{1,2,0:T(8,128)(2,1)}, u32[]{:S(2)}, u32[]{:S(2)}) async-start(bf16[8,128,1024]{1,2,0:T(8,128)(2,1)} %stack.26), calls=%async_computation | async-start | bytes 4194304 | tf_op jit(solution)/shard_map/all_to_all | solution.py:45
  21.8 45.6 %all-to-all-done = bf16[8,128,1024]{1,2,0:T(8,128)(2,1)} async-done(((bf16[8,128,1024]{1,2,0:T(8,128)(2,1)}), bf16[8,128,1024]{1,2,0:T(8,128)(2,1)}, u32[]{:S(2)}, u32[]{:S(2)}) %all-to-all-start) | async-done | bytes 2097184 | tf_op jit(solution)/shard_map/all_to_all | solution.py:45
  67.4 10.4 %all-to-all-start.1 = ((bf16[128,16,512]{0,2,1:T(8,128)(2,1)}), bf16[128,16,512]{0,2,1:T(8,128)(2,1)S(1)}, u32[]{:S(2)}, u32[]{:S(2)}) async-start(bf16[128,16,512]{0,2,1:T(8,128)(2,1)} %bitcast.4), calls=%async_computation.1 | async-start | bytes 4194304 | tf_op jit(solution)/shard_map/all_to_all | solution.py:47
  77.9 38.7 %while.42 = (s32[]{:T(128)}, s32[]{:T(128)}, s32[16]{0:T(128)S(1)}, s32[16]{0:T(128)S(1)}, s32[]{:T(128)}, /*index=5*/s32[]{:T(128)}, s32[]{:T(128)}) while((s32[]{:T(128)}, s32[]{:T(128)}, s32[16]{0:T(128)S(1)}, s32[16]{0:T(128)S(1)}, s32[]{:T(128)}, /*index=5*/s32[]{:T(128)}, s32[]{:T(128)}) %tuple.69), condition=%wide.region_2.3_spmd.clone, body=%wide.region_1.2_spmd.clone.sunk | while | flops 70 | bytes 273 | solution.py:60
  116.7 10.4 %all-to-all-done.1 = bf16[128,16,512]{0,2,1:T(8,128)(2,1)S(1)} async-done(((bf16[128,16,512]{0,2,1:T(8,128)(2,1)}), bf16[128,16,512]{0,2,1:T(8,128)(2,1)S(1)}, u32[]{:S(2)}, u32[]{:S(2)}) %all-to-all-start.1) | async-done | bytes 2097184 | tf_op jit(solution)/shard_map/all_to_all | solution.py:47
  127.1 1.3 copy-done.7
  128.4 2.9 copy.23
  131.3 2.0 fusion.48
  133.3 60.2 %all-reduce.7 = bf16[2048,256]{1,0:T(8,128)(2,1)} all-reduce(f32[2048,256]{1,0:T(8,128)} %fusion.48), channel_id=1, replica_groups=mesh['dp'=4,'seq'=16,'tensor'=8] {'seq'}, use_global_device_ids=true, to_apply=%region_0.0 | all-reduce | flops 524288 | bytes 3145728 | tf_op jit(solution)/shard_map/psum | solution.py:49
  193.5 2.2 squeeze.41
  195.6 3.2 fusion.47
  198.8 1.8 copy.42
  200.7 39.9 %while.43 = (s32[]{:T(128)}, f32[2048,128]{1,0:T(8,128)}, f32[2048,128]{1,0:T(8,128)}, bf16[2,128,4,128]{3,1,2,0:T(8,128)(2,1)}, f32[2,128,4,128]{3,1,2,0:T(8,12...) while((s32[]{:T(128)}, f32[2048,128]{1,0:T(8,128)}, ...), condition=%wide.region_7.8_spmd.clone, body=%wide.region_3.7_spmd.clone.sunk | while | flops 1626342912 | bytes 79985504 | solution.py:90
  201.7 1.9 fusion.91
  203.5 1.9 copy-done.2
  207.2 1.8 multiply_reduce_fusion.2
  209.0 4.5 %fusion.93 = bf16[4,128,2048]{2,1,0:T(8,128)(2,1)} fusion(f32[4,128]{1,0:T(4,128)S(1)} %bitcast.170, f32[4,128,2048]{2,1,0:T(8,128)} %copy-done.2, f32[4,128]{1,0:T(4,128)} %copy-done.13, bf16[2048,128]{0,1:T(8,128)(2,1)} %get-tuple-element.396, bf16[1,128,4,128]{1,3,2,0:T(8,128)(2,1)S(1)} %constant_dynamic-slice_fusion.3), kind=kOutput, calls=%fused_computation.9.clone.1 | convolution fusion | flops 273678336 | bytes 6950912 | tf_op jit(solution)/shard_map/while/body/eval_jaxpr/while/body/eval_jaxpr/thd,jd->htj/dot_general | solution.py:22
  213.6 3.5 fusion.94
  221.5 1.9 fusion.91
  223.4 1.9 copy-done.2
  227.0 1.8 multiply_reduce_fusion.2
  228.9 4.5 %fusion.93 = bf16[4,128,2048]{2,1,0:T(8,128)(2,1)} fusion(f32[4,128]{1,0:T(4,128)S(1)} %bitcast.170, f32[4,128,2048]{2,1,0:T(8,128)} %copy-done.2, f32[4,128]{1,0:T(4,128)} %copy-done.13, bf16[2048,128]{0,1:T(8,128)(2,1)} %get-tuple-element.396, bf16[1,128,4,128]{1,3,2,0:T(8,128)(2,1)S(1)} %constant_dynamic-slice_fusion.3), kind=kOutput, calls=%fused_computation.9.clone.1 | convolution fusion | flops 273678336 | bytes 6950912 | tf_op jit(solution)/shard_map/while/body/eval_jaxpr/while/body/eval_jaxpr/thd,jd->htj/dot_general | solution.py:22
  233.4 3.8 fusion.94
  240.6 1.6 copy.32
  242.2 1.4 copy.31
  244.8 114.9 %all-reduce.4.cloned.1.call-done = bf16[2048,256]{0,1:T(8,128)(2,1)} async-done(((bf16[2048,256]{0,1:T(8,128)(2,1)}), bf16[2048,256]{0,1:T(8,128)(2,1)}) %all-reduce.4.cloned.1.call-update) | async-done | bytes 1048592 | tf_op jit(solution)/shard_map/psum | solution.py:97
  359.7 2.7 fusion.37
  363.8 1.2 copy.29
  365.8 50.2 %all-reduce.6.cloned.1.call-done = f32[512,256]{0,1:T(8,128)} async-done(((f32[512,256]{0,1:T(8,128)}), f32[512,256]{0,1:T(8,128)}) %all-reduce.6.cloned.1.call-update) | async-done | bytes 524304 | tf_op jit(solution)/shard_map/psum | solution.py:101
  416.1 2.0 copy.33
  (110 shorter events, 26.5 us)
Async XLA Ops:
  7.2 124.1 %copy-start = (bf16[512,256]{1,0:T(8,128)(2,1)S(1)}, bf16[512,256]{1,0:T(8,128)(2,1)}, u32[]{:S(2)}) copy-start(bf16[512,256]{1,0:T(8,128)(2,1)} %param.11) | copy-start | bytes 786436
  7.2 12.8 %copy-start.11 = (bf16[128,1024]{1,0:T(8,128)(2,1)S(1)}, bf16[128,1024]{1,0:T(8,128)(2,1)}, u32[]{:S(2)}) copy-start(bf16[128,1024]{1,0:T(8,128)(2,1)} %param.13) | copy-start | bytes 786436
  7.2 13.7 %copy-start.12 = (bf16[128,1024]{1,0:T(8,128)(2,1)S(1)}, bf16[128,1024]{1,0:T(8,128)(2,1)}, u32[]{:S(2)}) copy-start(bf16[128,1024]{1,0:T(8,128)(2,1)} %param.10) | copy-start | bytes 786436
  7.2 13.9 %copy-start.14 = (s32[1,16]{1,0:T(1,128)S(1)}, s32[1,16]{1,0:T(1,128)}, u32[]{:S(2)}) copy-start(s32[1,16]{1,0:T(1,128)} %param.12) | copy-start | bytes 196
  10.0 57.4 %all-to-all-start = ((bf16[8,128,1024]{1,2,0:T(8,128)(2,1)}), bf16[8,128,1024]{1,2,0:T(8,128)(2,1)}, u32[]{:S(2)}, u32[]{:S(2)}) async-start(bf16[8,128,1024]{1,2,0:T(8,128)(2,1)} %stack.26), calls=%async_computation | async-start | bytes 4194304 | tf_op jit(solution)/shard_map/all_to_all | solution.py:45
  67.4 59.7 %all-to-all-start.1 = ((bf16[128,16,512]{0,2,1:T(8,128)(2,1)}), bf16[128,16,512]{0,2,1:T(8,128)(2,1)S(1)}, u32[]{:S(2)}, u32[]{:S(2)}) async-start(bf16[128,16,512]{0,2,1:T(8,128)(2,1)} %bitcast.4), calls=%async_computation.1 | async-start | bytes 4194304 | tf_op jit(solution)/shard_map/all_to_all | solution.py:47
  77.8 281.9 %all-reduce.4.cloned.1.call-start = ((), (), s32[]{:S(2)}) async-start(), calls=%async_computation.2 | async-start | bytes 2097152 | tf_op jit(solution)/shard_map/psum | solution.py:97
  127.0 1.3 copy-start.7
  131.2 62.2 %copy-start.5 = (bf16[16,128,512]{2,1,0:T(8,128)(2,1)}, bf16[16,128,512]{2,1,0:T(8,128)(2,1)S(1)}, u32[]{:S(2)}) copy-start(bf16[16,128,512]{2,1,0:T(8,128)(2,1)S(1)} %copy.23) | copy-start | bytes 6291460
  203.5 2.0 copy-start.2
  203.5 2.6 copy-start.13
  213.6 3.6 copy-start.1
  213.6 3.6 copy-start.8
  213.6 4.3 %copy-start.3 = (f32[2048,128]{1,0:T(8,128)S(1)}, f32[2048,128]{1,0:T(8,128)}, u32[]{:S(2)}) copy-start(f32[2048,128]{1,0:T(8,128)} %get-tuple-element.376) | copy-start | bytes 3145732 | tf_op jit(solution)/shard_map/while/body/eval_jaxpr/while
  217.8 2.0 copy-start.9
  218.9 1.0 copy-start.4
  223.3 2.0 copy-start.2
  223.3 2.6 copy-start.13
  233.4 3.8 copy-start.1
  233.4 3.8 copy-start.8
  233.4 4.5 %copy-start.3 = (f32[2048,128]{1,0:T(8,128)S(1)}, f32[2048,128]{1,0:T(8,128)}, u32[]{:S(2)}) copy-start(f32[2048,128]{1,0:T(8,128)} %get-tuple-element.376) | copy-start | bytes 3145732 | tf_op jit(solution)/shard_map/while/body/eval_jaxpr/while
  237.9 2.0 copy-start.9
  239.0 1.0 copy-start.4
  240.6 119.1 %copy-start.6 = (bf16[16,128,512]{2,1,0:T(8,128)(2,1)S(1)}, bf16[16,128,512]{2,1,0:T(8,128)(2,1)}, u32[]{:S(2)}) copy-start(bf16[16,128,512]{2,1,0:T(8,128)(2,1)} %copy-done.5) | copy-start | bytes 6291460
  244.7 117.7 %copy-start.10 = (f32[2,128,4,128]{3,1,2,0:T(8,128)S(1)}, f32[2,128,4,128]{3,1,2,0:T(8,128)}, u32[]{:S(2)}) copy-start(f32[2,128,4,128]{3,1,2,0:T(8,128)} %get-tuple-element.111) | copy-start | bytes 1572868
  244.8 171.3 %all-reduce.6.cloned.1.call-start = ((), (), s32[]{:S(2)}) async-start(), calls=%async_computation.3 | async-start | bytes 1048576 | tf_op jit(solution)/shard_map/psum | solution.py:101
Sparse Core Ops, SparseCore 0:
  244.9 114.7 all-reduce.3
  362.6 53.4 all-reduce.5
